TPU v7x, 32 devices: a whole 2x2x4 slice. The times are simulated.
32 devices in a mesh: blk: 16 (over z, x, core), rep: 2 (over y).
Axes of the slice: x: 2, y: 2, z: 4, core: 2. Of those that a mesh axis runs over, the one named last changes fastest.
Arguments:
- features: bfloat16 [4096, 128], P(('blk', 'rep')), may hold values from -6 to 6
- tile_mask: int32 [32, 32], P('blk'), may hold values 0 or 1
- multiplicity: int32 [32, 32], P('blk'), may hold values from 1 to 4
- w_query: bfloat16 [128, 128], replicated, may hold values from -0.5 to 0.5
- w_value: bfloat16 [128, 128], replicated, may hold values from -0.5 to 0.5
Outputs:
- updated: bfloat16 [4096, 128], P(('blk', 'rep'))
All inputs are finite; a program needn't handle non-finite values. No bound on the sum of `tile_mask` on one device may be relied on, other than what follows from the above.
Results may differ from a plain program's by a relative error of at most 0.0057.
Values may be sent and summed in bfloat16 or wider, within the bound.
A program may use at most 64 MiB of HBM per device.

v0:
```python
import math
import jax
import jax.numpy as jnp
from jax import lax
from jax.sharding import PartitionSpec as P

TILE = 128


def body(features, tile_mask, multiplicity, w_query, w_value):
    src_rows = features.shape[0]
    cycle_count = lax.axis_size("blk")
    rep_count = lax.axis_size("rep")
    rep_index = lax.axis_index("rep")
    own_query = jnp.dot(features, w_query, preferred_element_type=jnp.float32).astype(jnp.bfloat16)
    queries = lax.all_gather(own_query, "rep", axis=0, tiled=True)
    tgt_rows = queries.shape[0]
    tgt_tiles = tgt_rows // TILE
    src_tiles = src_rows // TILE
    factor = (tile_mask * multiplicity).astype(jnp.float32)
    factor = factor.reshape(tgt_tiles, cycle_count, rep_count, src_tiles)
    factor = lax.dynamic_index_in_dim(factor, rep_index, 2, keepdims=False)
    root_scale = 1.0 / features.shape[1] ** 0.5

    def absorb_tiles(partial_value, source, tile_factor):
        count_rows = source.shape[0]
        scores = (
            lax.dot_general(
                queries, source, (((1,), (1,)), ((), ())), preferred_element_type=jnp.float32
            )
            * root_scale
        )
        scores = jnp.where(scores > 0, scores, 0.2 * scores)
        weights = (
            scores.reshape(tgt_tiles, TILE, count_rows // TILE, TILE)
            * tile_factor[:, None, :, None]
        )
        weights = weights.reshape(tgt_rows, count_rows).astype(jnp.bfloat16)
        return partial_value + jnp.dot(weights, source, preferred_element_type=jnp.float32)

    start = jnp.zeros((tgt_rows, features.shape[1]), jnp.float32)
    flat_factor = factor.reshape(tgt_tiles, cycle_count * src_tiles)
    piece = lax.all_gather(features, "blk", axis=0, tiled=True)
    piece_rows = piece.shape[0]
    step_rows = math.gcd(piece_rows, max(src_rows, 1024))
    step_count = piece_rows // step_rows
    piece_blocks = piece.reshape(step_count, step_rows, piece.shape[1])

    def one_part(carry, index_pair):
        part_rows, part_index = index_pair
        first_tile = part_index * step_rows // TILE
        tile_factor = lax.dynamic_slice_in_dim(flat_factor, first_tile, step_rows // TILE, 1)
        return (absorb_tiles(carry, part_rows, tile_factor), None)

    result, unused = lax.scan(
        one_part, start, (piece_blocks, jnp.arange(step_count, dtype=jnp.int32))
    )
    partial_value = result
    summed = lax.psum_scatter(partial_value, "rep", scatter_dimension=0, tiled=True)
    total_verts = src_rows * cycle_count * rep_count
    aggregate = (summed * (2.0 * total_verts) ** (-0.5)).astype(jnp.bfloat16)
    mixed = jnp.dot(aggregate, w_value, preferred_element_type=jnp.float32)
    return (features.astype(jnp.float32) + mixed).astype(jnp.bfloat16)


def solution(mesh):
    in_specs = (P(("blk", "rep"), None), P("blk", None), P("blk", None), P(), P())
    out_specs = P(("blk", "rep"), None)
    return jax.shard_map(body, mesh=mesh, in_specs=in_specs, out_specs=out_specs, check_vma=False)
```

profile of v0, /device:TPU:0, one launch (start us, length us, event | category | flops | bytes accessed | tf_op | source)
XLA Modules:
  0.0 58.8 jit_solution(14389451639451653202)
XLA Ops:
  6.5 0.0 copy-start
  6.5 0.0 reduce-scatter.2.cloned.1.call-start
  6.5 0.0 copy-start.5
  6.5 0.0 copy-start.4
  6.6 0.7 %copy-done.5 = s32[2,32]{1,0:T(2,128)S(1)} copy-done((s32[2,32]{1,0:T(2,128)S(1)}, s32[2,32]{1,0:T(2,128)}, u32[]{:S(2)}) %copy-start.5) | copy-done | bytes 280
  7.2 0.0 copy-done.4
  7.3 0.1 reshape.20
  7.3 0.0 copy-start.1
  7.3 0.1 constant_dynamic-slice_fusion.1
  7.4 0.2 copy.8
  7.6 0.5 copy-done.1
  8.1 24.6 %all_gather.6 = bf16[2048,128]{1,0:T(8,128)(2,1)S(1)} all-gather(bf16[128,128]{1,0:T(8,128)(2,1)S(1)} %copy-done.1), channel_id=1, replica_groups=mesh['blk'=16,'rep'=2] {'blk'}, dimensions={0}, use_global_device_ids=true | all-gather | bytes 557056 | tf_op jit(solution)/shard_map/all_gather | solution.py:43
  32.7 0.0 copy-done
  32.7 0.1 convolution_convert_fusion
  32.8 4.6 %all_gather.7 = bf16[256,128]{1,0:T(8,128)(2,1)S(1)} all-gather(bf16[128,128]{1,0:T(8,128)(2,1)S(1)} %convolution_convert_fusion), channel_id=1, replica_groups=mesh['blk'=16,'rep'=2] {'rep'}, dimensions={0}, use_global_device_ids=true | all-gather | bytes 98304 | tf_op jit(solution)/shard_map/all_gather | solution.py:16
  37.4 4.4 %while.13 = (s32[]{:T(128)}, f32[256,128]{1,0:T(8,128)S(1)}, bf16[2,1024,128]{2,1,0:T(8,128)(2,1)S(1)}, bf16[256,128]{1,0:T(8,128)(2,1)S(1)}, s32[2]{0:T(128)S(1...) while((s32[]{:T(128)}, f32[256,128]{1,0:T(8,128)S(1)}, ...), condition=%wide.region_1.2_spmd.clone, body=%wide.region_0.1_spmd.clone.sunk | while | flops 135856144 | bytes 2950683 | solution.py:55
  37.4 0.6 dynamic_slice.44
  38.6 0.3 mul.98
  38.9 0.7 %convolution_add_fusion.3 = f32[256,128]{1,0:T(8,128)S(1)} fusion(f32[128,8,2,128]{3,2,1,0:T(2,128)S(1)} %bitcast.43, bf16[256,128]{1,0:T(8,128)(2,1)S(1)} %get-tuple-element.196, bf16[2,1024,128]{2,1,0:T(8,128)(2,1)S(1)} %get-tuple-element.195, s32[]{:T(128)} %get-tuple-element.180, f32[256,128]{1,0:T(8,128)S(1)} %get-tuple-element.181, pred[]{:T(512)S(6)} %compare.9), kind=kOutput, calls=%fused_computation.1.clone.1 | convolution fusion | flops 135856128 | bytes 1901569 | tf_op jit(solution)/shard_map/while/body/eval_jaxpr/dot_general | solution.py:39
  39.6 0.6 dynamic_slice.44
  40.8 0.3 mul.98
  41.2 0.7 %convolution_add_fusion.3 = f32[256,128]{1,0:T(8,128)S(1)} fusion(f32[128,8,2,128]{3,2,1,0:T(2,128)S(1)} %bitcast.43, bf16[256,128]{1,0:T(8,128)(2,1)S(1)} %get-tuple-element.196, bf16[2,1024,128]{2,1,0:T(8,128)(2,1)S(1)} %get-tuple-element.195, s32[]{:T(128)} %get-tuple-element.180, f32[256,128]{1,0:T(8,128)S(1)} %get-tuple-element.181, pred[]{:T(512)S(6)} %compare.9), kind=kOutput, calls=%fused_computation.1.clone.1 | convolution fusion | flops 135856128 | bytes 1901569 | tf_op jit(solution)/shard_map/while/body/eval_jaxpr/dot_general | solution.py:39
  41.8 0.0 copy-start.2
  41.9 0.0 copy-start.3
  41.9 0.6 %copy-done.2 = f32[256,128]{1,0:T(8,128)} copy-done((f32[256,128]{1,0:T(8,128)}, f32[256,128]{1,0:T(8,128)S(1)}, u32[]{:S(2)}) %copy-start.2) | copy-done | bytes 131096
  42.5 0.0 reduce-scatter.2.cloned.1.call-update
  42.5 7.8 %reduce-scatter.2.cloned.1.call-done = f32[128,128]{1,0:T(8,128)} async-done(((f32[256,128]{1,0:T(8,128)}), f32[128,128]{1,0:T(8,128)}) %reduce-scatter.2.cloned.1.call-update) | async-done | bytes 65552 | tf_op jit(solution)/shard_map/reduce_scatter | solution.py:59
  50.3 0.0 copy-done.3
  50.3 1.6 %fusion.14 = bf16[128,128]{1,0:T(8,128)(2,1)} fusion(bf16[128,128]{1,0:T(8,128)(2,1)S(1)} %copy-done.3, bf16[128,128]{1,0:T(8,128)(2,1)S(1)} %copy-done.1, f32[128,128]{1,0:T(8,128)} %reduce-scatter.2.cloned.1.call-done), kind=kOutput, calls=%fused_computation.15 | convolution fusion | flops 4276224 | bytes 163840 | tf_op jit(solution)/shard_map/dot_general | solution.py:62
  (5 shorter events, 0.0 us)
Async XLA Ops:
  6.5 26.2 %copy-start = (bf16[128,128]{1,0:T(8,128)(2,1)S(1)}, bf16[128,128]{1,0:T(8,128)(2,1)}, u32[]{:S(2)}) copy-start(bf16[128,128]{1,0:T(8,128)(2,1)} %param.10) | copy-start | bytes 98308
  6.5 43.8 %reduce-scatter.2.cloned.1.call-start = ((), (), s32[]{:S(2)}) async-start(), calls=%async_computation.1 | async-start | bytes 196608 | tf_op jit(solution)/shard_map/reduce_scatter | solution.py:59
  6.5 0.7 %copy-start.5 = (s32[2,32]{1,0:T(2,128)S(1)}, s32[2,32]{1,0:T(2,128)}, u32[]{:S(2)}) copy-start(s32[2,32]{1,0:T(2,128)} %param.9) | copy-start | bytes 772
  6.5 0.7 %copy-start.4 = (s32[2,32]{1,0:T(2,128)S(1)}, s32[2,32]{1,0:T(2,128)}, u32[]{:S(2)}) copy-start(s32[2,32]{1,0:T(2,128)} %param.8) | copy-start | bytes 772
  7.3 0.8 %copy-start.1 = (bf16[128,128]{1,0:T(8,128)(2,1)S(1)}, bf16[128,128]{1,0:T(8,128)(2,1)}, u32[]{:S(2)}) copy-start(bf16[128,128]{1,0:T(8,128)(2,1)} %param.7) | copy-start | bytes 98308
  41.8 0.7 %copy-start.2 = (f32[256,128]{1,0:T(8,128)}, f32[256,128]{1,0:T(8,128)S(1)}, u32[]{:S(2)}) copy-start(f32[256,128]{1,0:T(8,128)S(1)} %get-tuple-element.84) | copy-start | bytes 393220
  41.9 8.5 %copy-start.3 = (bf16[128,128]{1,0:T(8,128)(2,1)S(1)}, bf16[128,128]{1,0:T(8,128)(2,1)}, u32[]{:S(2)}) copy-start(bf16[128,128]{1,0:T(8,128)(2,1)} %param.11) | copy-start | bytes 98308
Sparse Core Ops, SparseCore 0:
  42.6 7.6 reduce-scatter.1
where the time goes:
time: 59.1 us; the launch traced here: 58.8 us
  blocking collectives  29.2 us (49%)
  between operations  13.4 us (23%)
  waiting for transfers between devices  7.82 us (13%)
  local copies, waits for them, and re-layouts  4.05 us (7%)
  matrix products  3.05 us (5%)
  loops' own time  1.24 us (2%)
    all_gather x1, blocking collectives, body(): piece = lax.all_gather(features, 'blk', axis=0, tiled=True)  24.6 us
    reduce_scatter x1, waiting for transfers between devices, body(): lax.psum_scatter(partial_value, 'rep', scatter_dimension=0, tiled=True)  7.8 us
    all_gather x1, blocking collectives, body(): queries = lax.all_gather(own_query, 'rep', axis=0, tiled=True)  4.58 us
    unnamed x13, local copies, waits for them, and re-layouts  2.02 us
    dot_general x1, matrix products, body(): mixed = jnp.dot(aggregate, w_value, preferred_element_type=jnp.float32)  1.59 us
    dot_general x2, matrix products, absorb_tiles(): jnp.dot(weights, source, preferred_element_type=jnp.float32)  1.33 us
    another operation x1, loops' own time, body(): lax.scan(one_part, start, (piece_blocks, jnp.arange(step_count, dtype=jnp...  1.24 us
  transfers between devices with their start and end apart: 1, of which 1 were waited for; matrix products, arithmetic and copies ran while one was open for 0% of the time, Pallas kernels for 0%

commit v1 on v0

--- a/solution.py
+++ b/solution.py
@@ -5,6 +5,19 @@
 from jax.sharding import PartitionSpec as P
 
 TILE = 128
+
+
+def ring_gather(x, axis, dim):
+    size, index, rows = (lax.axis_size(axis), lax.axis_index(axis), x.shape[dim])
+    upward = [(i, (i + 1) % size) for i in range(size)]
+    out = jnp.zeros((*x.shape[:dim], size * rows, *x.shape[dim + 1 :]), x.dtype)
+    carried = x
+    for step in range(size):
+        source = (index - step) % size
+        out = lax.dynamic_update_slice_in_dim(out, carried, source * rows, axis=dim)
+        if step < size - 1:
+            carried = lax.ppermute(carried, axis, upward)
+    return out
 
 
 def body(features, tile_mask, multiplicity, w_query, w_value):
@@ -40,7 +53,7 @@
 
     start = jnp.zeros((tgt_rows, features.shape[1]), jnp.float32)
     flat_factor = factor.reshape(tgt_tiles, cycle_count * src_tiles)
-    piece = lax.all_gather(features, "blk", axis=0, tiled=True)
+    piece = ring_gather(features, "blk", 0)
     piece_rows = piece.shape[0]
     step_rows = math.gcd(piece_rows, max(src_rows, 1024))
     step_count = piece_rows // step_rows

time: 59.1 us -> 121 us (2.05)
  waiting for transfers between devices: 7.82 us -> 91.9 us
  blocking collectives: 29.2 us -> 5.07 us
  starting transfers between devices: 0.01 us -> 1.38 us
    ppermute x0 -> x15, waiting for transfers between devices: none -> 83.6 us  [ring_gather(): carried = lax.ppermute(carried, axis, upward)]
    all_gather x1 -> x0, blocking collectives: 24.6 us -> none  [body(): piece = lax.all_gather(features, 'blk', axis=0, tiled=True)]
    ppermute x0 -> x15, starting transfers between devices: none -> 1.37 us  [ring_gather(): carried = lax.ppermute(carried, axis, upward)]
  transfers between devices with their start and end apart: 1 -> 16, of which waited for: 1 -> 16; matrix products, arithmetic and copies ran while one was open for 0% -> 1% of each run, Pallas kernels for 0% -> 0%
where the time goes in v1:
time: 121 us; the launch traced here: 120 us
  waiting for transfers between devices  91.9 us (76%)
  between operations  13.8 us (11%)
  blocking collectives  5.07 us (4%)
  local copies, waits for them, and re-layouts  3.86 us (3%)
  matrix products  3.07 us (3%)
  loops' own time  1.4 us (1%)
  starting transfers between devices  1.38 us (1%)
    ppermute x15, waiting for transfers between devices, ring_gather(): carried = lax.ppermute(carried, axis, upward)  83.6 us
    reduce_scatter x1, waiting for transfers between devices, body(): lax.psum_scatter(partial_value, 'rep', scatter_dimension=0, tiled=True)  8.25 us
    all_gather x1, blocking collectives, body(): queries = lax.all_gather(own_query, 'rep', axis=0, tiled=True)  5.07 us
  transfers between devices with their start and end apart: 16, of which 16 were waited for; matrix products, arithmetic and copies ran while one was open for 1% of the time, Pallas kernels for 0%

profile of v1, /device:TPU:0, one launch (start us, length us, event | category | flops | bytes accessed | tf_op | source)
XLA Modules:
  0.0 120.4 jit_solution(10581171954243351530)
XLA Ops:
  6.5 0.0 copy-start
  6.5 0.0 copy-start.1
  6.5 0.0 reduce-scatter.2.cloned.1.call-start
  6.5 0.5 collective-permute-start
  7.0 0.0 copy-start.5
  7.0 0.0 copy-start.4
  7.0 0.7 copy-done.5
  7.7 0.0 copy-done.4
  7.7 0.1 reshape.20
  7.8 0.0 copy-done
  7.8 0.0 copy-done.1
  7.8 0.1 convolution_convert_fusion
  8.0 0.1 broadcast_in_dim.8
  8.1 0.1 constant_dynamic-slice_fusion.1
  8.4 0.2 copy.8
  8.6 5.1 %all_gather.3 = bf16[256,128]{1,0:T(8,128)(2,1)S(1)} all-gather(bf16[128,128]{1,0:T(8,128)(2,1)S(1)} %convolution_convert_fusion), channel_id=1, replica_groups=mesh['blk'=16,'rep'=2] {'rep'}, dimensions={0}, use_global_device_ids=true | all-gather | bytes 98304 | tf_op jit(solution)/shard_map/all_gather | solution.py:29
  13.7 0.1 collective-permute-done
  13.8 0.8 collective-permute-start.1
  14.7 5.2 %collective-permute-done.1 = bf16[128,128]{1,0:T(8,128)(2,1)S(1)} collective-permute-done((bf16[128,128]{1,0:T(8,128)(2,1)S(1)}, bf16[128,128]{1,0:T(8,128)(2,1)S(1)}, u32[]{:S(2)}, u32[]{:S(2)}) %collective-permute-start.1) | collective-permute-done | bytes 32800 | tf_op jit(solution)/shard_map/ppermute | solution.py:19
  19.9 0.0 collective-permute-start.2
  19.9 6.0 %collective-permute-done.2 = bf16[128,128]{1,0:T(8,128)(2,1)S(1)} collective-permute-done((bf16[128,128]{1,0:T(8,128)(2,1)S(1)}, bf16[128,128]{1,0:T(8,128)(2,1)S(1)}, u32[]{:S(2)}, u32[]{:S(2)}) %collective-permute-start.2) | collective-permute-done | bytes 32800 | tf_op jit(solution)/shard_map/ppermute | solution.py:19
  25.9 0.0 collective-permute-start.3
  25.9 6.0 %collective-permute-done.3 = bf16[128,128]{1,0:T(8,128)(2,1)S(1)} collective-permute-done((bf16[128,128]{1,0:T(8,128)(2,1)S(1)}, bf16[128,128]{1,0:T(8,128)(2,1)S(1)}, u32[]{:S(2)}, u32[]{:S(2)}) %collective-permute-start.3) | collective-permute-done | bytes 32800 | tf_op jit(solution)/shard_map/ppermute | solution.py:19
  31.9 0.0 collective-permute-start.4
  31.9 6.0 %collective-permute-done.4 = bf16[128,128]{1,0:T(8,128)(2,1)S(1)} collective-permute-done((bf16[128,128]{1,0:T(8,128)(2,1)S(1)}, bf16[128,128]{1,0:T(8,128)(2,1)S(1)}, u32[]{:S(2)}, u32[]{:S(2)}) %collective-permute-start.4) | collective-permute-done | bytes 32800 | tf_op jit(solution)/shard_map/ppermute | solution.py:19
  38.0 0.0 collective-permute-start.5
  38.0 6.0 %collective-permute-done.5 = bf16[128,128]{1,0:T(8,128)(2,1)S(1)} collective-permute-done((bf16[128,128]{1,0:T(8,128)(2,1)S(1)}, bf16[128,128]{1,0:T(8,128)(2,1)S(1)}, u32[]{:S(2)}, u32[]{:S(2)}) %collective-permute-start.5) | collective-permute-done | bytes 32800 | tf_op jit(solution)/shard_map/ppermute | solution.py:19
  44.0 0.0 collective-permute-start.6
  44.0 6.0 %collective-permute-done.6 = bf16[128,128]{1,0:T(8,128)(2,1)S(1)} collective-permute-done((bf16[128,128]{1,0:T(8,128)(2,1)S(1)}, bf16[128,128]{1,0:T(8,128)(2,1)S(1)}, u32[]{:S(2)}, u32[]{:S(2)}) %collective-permute-start.6) | collective-permute-done | bytes 32800 | tf_op jit(solution)/shard_map/ppermute | solution.py:19
  50.0 0.0 collective-permute-start.7
  50.1 6.0 %collective-permute-done.7 = bf16[128,128]{1,0:T(8,128)(2,1)S(1)} collective-permute-done((bf16[128,128]{1,0:T(8,128)(2,1)S(1)}, bf16[128,128]{1,0:T(8,128)(2,1)S(1)}, u32[]{:S(2)}, u32[]{:S(2)}) %collective-permute-start.7) | collective-permute-done | bytes 32800 | tf_op jit(solution)/shard_map/ppermute | solution.py:19
  56.1 0.0 collective-permute-start.8
  56.1 6.0 %collective-permute-done.8 = bf16[128,128]{1,0:T(8,128)(2,1)S(1)} collective-permute-done((bf16[128,128]{1,0:T(8,128)(2,1)S(1)}, bf16[128,128]{1,0:T(8,128)(2,1)S(1)}, u32[]{:S(2)}, u32[]{:S(2)}) %collective-permute-start.8) | collective-permute-done | bytes 32800 | tf_op jit(solution)/shard_map/ppermute | solution.py:19
  62.1 0.0 collective-permute-start.9
  62.1 6.0 %collective-permute-done.9 = bf16[128,128]{1,0:T(8,128)(2,1)S(1)} collective-permute-done((bf16[128,128]{1,0:T(8,128)(2,1)S(1)}, bf16[128,128]{1,0:T(8,128)(2,1)S(1)}, u32[]{:S(2)}, u32[]{:S(2)}) %collective-permute-start.9) | collective-permute-done | bytes 32800 | tf_op jit(solution)/shard_map/ppermute | solution.py:19
  68.2 0.0 collective-permute-start.10
  68.2 6.0 %collective-permute-done.10 = bf16[128,128]{1,0:T(8,128)(2,1)S(1)} collective-permute-done((bf16[128,128]{1,0:T(8,128)(2,1)S(1)}, bf16[128,128]{1,0:T(8,128)(2,1)S(1)}, u32[]{:S(2)}, u32[]{:S(2)}) %collective-permute-start.10) | collective-permute-done | bytes 32800 | tf_op jit(solution)/shard_map/ppermute | solution.py:19
  74.2 0.0 collective-permute-start.11
  74.2 6.0 %collective-permute-done.11 = bf16[128,128]{1,0:T(8,128)(2,1)S(1)} collective-permute-done((bf16[128,128]{1,0:T(8,128)(2,1)S(1)}, bf16[128,128]{1,0:T(8,128)(2,1)S(1)}, u32[]{:S(2)}, u32[]{:S(2)}) %collective-permute-start.11) | collective-permute-done | bytes 32800 | tf_op jit(solution)/shard_map/ppermute | solution.py:19
  80.2 0.0 collective-permute-start.12
  80.2 6.0 %collective-permute-done.12 = bf16[128,128]{1,0:T(8,128)(2,1)S(1)} collective-permute-done((bf16[128,128]{1,0:T(8,128)(2,1)S(1)}, bf16[128,128]{1,0:T(8,128)(2,1)S(1)}, u32[]{:S(2)}, u32[]{:S(2)}) %collective-permute-start.12) | collective-permute-done | bytes 32800 | tf_op jit(solution)/shard_map/ppermute | solution.py:19
  86.3 0.0 collective-permute-start.13
  86.3 6.0 %collective-permute-done.13 = bf16[128,128]{1,0:T(8,128)(2,1)S(1)} collective-permute-done((bf16[128,128]{1,0:T(8,128)(2,1)S(1)}, bf16[128,128]{1,0:T(8,128)(2,1)S(1)}, u32[]{:S(2)}, u32[]{:S(2)}) %collective-permute-start.13) | collective-permute-done | bytes 32800 | tf_op jit(solution)/shard_map/ppermute | solution.py:19
  92.3 0.0 collective-permute-start.14
  92.3 6.0 %collective-permute-done.14 = bf16[128,128]{1,0:T(8,128)(2,1)S(1)} collective-permute-done((bf16[128,128]{1,0:T(8,128)(2,1)S(1)}, bf16[128,128]{1,0:T(8,128)(2,1)S(1)}, u32[]{:S(2)}, u32[]{:S(2)}) %collective-permute-start.14) | collective-permute-done | bytes 32800 | tf_op jit(solution)/shard_map/ppermute | solution.py:19
  98.4 4.7 %while.13 = (s32[]{:T(128)}, f32[256,128]{1,0:T(8,128)S(1)}, bf16[2,1024,128]{2,1,0:T(8,128)(2,1)S(1)}, bf16[256,128]{1,0:T(8,128)(2,1)S(1)}, s32[2]{0:T(128)S(1...) while((s32[]{:T(128)}, f32[256,128]{1,0:T(8,128)S(1)}, ...), condition=%wide.region_1.2_spmd.clone, body=%wide.region_0.1_spmd.clone.sunk | while | flops 135856144 | bytes 2950683 | solution.py:68
  98.4 0.6 dynamic_slice.44
  99.7 0.3 mul.162
  100.0 0.7 convolution_add_fusion.3
  100.7 0.6 dynamic_slice.44
  102.0 0.3 mul.162
  102.4 0.7 convolution_add_fusion.3
  103.0 0.0 copy-start.2
  103.1 0.0 copy-start.3
  103.1 0.6 copy-done.2
  103.7 0.0 reduce-scatter.2.cloned.1.call-update
  103.7 8.3 %reduce-scatter.2.cloned.1.call-done = f32[128,128]{1,0:T(8,128)} async-done(((f32[256,128]{1,0:T(8,128)}), f32[128,128]{1,0:T(8,128)}) %reduce-scatter.2.cloned.1.call-update) | async-done | bytes 65552 | tf_op jit(solution)/shard_map/reduce_scatter | solution.py:72
  112.0 0.0 copy-done.3
  112.0 1.6 %fusion.14 = bf16[128,128]{1,0:T(8,128)(2,1)} fusion(bf16[128,128]{1,0:T(8,128)(2,1)S(1)} %copy-done.3, bf16[128,128]{1,0:T(8,128)(2,1)S(1)} %copy-done.1, f32[128,128]{1,0:T(8,128)} %reduce-scatter.2.cloned.1.call-done), kind=kOutput, calls=%fused_computation.15 | convolution fusion | flops 4276224 | bytes 163840 | tf_op jit(solution)/shard_map/dot_general | solution.py:75
  (21 shorter events, 0.2 us)
Async XLA Ops:
  6.5 1.3 %copy-start = (bf16[128,128]{1,0:T(8,128)(2,1)S(1)}, bf16[128,128]{1,0:T(8,128)(2,1)}, u32[]{:S(2)}) copy-start(bf16[128,128]{1,0:T(8,128)(2,1)} %param.10) | copy-start | bytes 98308
  6.5 1.3 %copy-start.1 = (bf16[128,128]{1,0:T(8,128)(2,1)S(1)}, bf16[128,128]{1,0:T(8,128)(2,1)}, u32[]{:S(2)}) copy-start(bf16[128,128]{1,0:T(8,128)(2,1)} %param.7) | copy-start | bytes 98308
  6.5 105.4 %reduce-scatter.2.cloned.1.call-start = ((), (), s32[]{:S(2)}) async-start(), calls=%async_computation.1 | async-start | bytes 196608 | tf_op jit(solution)/shard_map/reduce_scatter | solution.py:72
  6.5 7.3 %collective-permute-start = (bf16[128,128]{1,0:T(8,128)(2,1)}, bf16[128,128]{1,0:T(8,128)(2,1)S(1)}, u32[]{:S(2)}, u32[]{:S(2)}) collective-permute-start(bf16[128,128]{1,0:T(8,128)(2,1)} %param.7), channel_id=1, source_target_pairs={{0,2},{2,4},{4,6},{6,8},{8,10},{10,12},{12,14},{14,16},{16,18},{18... | collective-permute-start | bytes 98312 | tf_op jit(solution)/shard_map/ppermute | solution.py:19
  7.0 0.7 copy-start.5
  7.0 0.7 copy-start.4
  13.8 6.0 %collective-permute-start.1 = (bf16[128,128]{1,0:T(8,128)(2,1)S(1)}, bf16[128,128]{1,0:T(8,128)(2,1)S(1)}, u32[]{:S(2)}, u32[]{:S(2)}) collective-permute-start(bf16[128,128]{1,0:T(8,128)(2,1)S(1)} %collective-permute-done), channel_id=1, source_target_pairs={{0,2},{2,4},{4,6},{6,8},{8,10},{10,12},{12,14},{14,16},{16,18},{18... | collective-permute-start | bytes 98312 | tf_op jit(solution)/shard_map/ppermute | solution.py:19
  19.9 6.0 %collective-permute-start.2 = (bf16[128,128]{1,0:T(8,128)(2,1)S(1)}, bf16[128,128]{1,0:T(8,128)(2,1)S(1)}, u32[]{:S(2)}, u32[]{:S(2)}) collective-permute-start(bf16[128,128]{1,0:T(8,128)(2,1)S(1)} %collective-permute-done.1), channel_id=1, source_target_pairs={{0,2},{2,4},{4,6},{6,8},{8,10},{10,12},{12,14},{14,16},{16,18},{18... | collective-permute-start | bytes 98312 | tf_op jit(solution)/shard_map/ppermute | solution.py:19
  25.9 6.0 %collective-permute-start.3 = (bf16[128,128]{1,0:T(8,128)(2,1)S(1)}, bf16[128,128]{1,0:T(8,128)(2,1)S(1)}, u32[]{:S(2)}, u32[]{:S(2)}) collective-permute-start(bf16[128,128]{1,0:T(8,128)(2,1)S(1)} %collective-permute-done.2), channel_id=1, source_target_pairs={{0,2},{2,4},{4,6},{6,8},{8,10},{10,12},{12,14},{14,16},{16,18},{18... | collective-permute-start | bytes 98312 | tf_op jit(solution)/shard_map/ppermute | solution.py:19
  31.9 6.0 %collective-permute-start.4 = (bf16[128,128]{1,0:T(8,128)(2,1)S(1)}, bf16[128,128]{1,0:T(8,128)(2,1)S(1)}, u32[]{:S(2)}, u32[]{:S(2)}) collective-permute-start(bf16[128,128]{1,0:T(8,128)(2,1)S(1)} %collective-permute-done.3), channel_id=1, source_target_pairs={{0,2},{2,4},{4,6},{6,8},{8,10},{10,12},{12,14},{14,16},{16,18},{18... | collective-permute-start | bytes 98312 | tf_op jit(solution)/shard_map/ppermute | solution.py:19
  38.0 6.0 %collective-permute-start.5 = (bf16[128,128]{1,0:T(8,128)(2,1)S(1)}, bf16[128,128]{1,0:T(8,128)(2,1)S(1)}, u32[]{:S(2)}, u32[]{:S(2)}) collective-permute-start(bf16[128,128]{1,0:T(8,128)(2,1)S(1)} %collective-permute-done.4), channel_id=1, source_target_pairs={{0,2},{2,4},{4,6},{6,8},{8,10},{10,12},{12,14},{14,16},{16,18},{18... | collective-permute-start | bytes 98312 | tf_op jit(solution)/shard_map/ppermute | solution.py:19
  44.0 6.0 %collective-permute-start.6 = (bf16[128,128]{1,0:T(8,128)(2,1)S(1)}, bf16[128,128]{1,0:T(8,128)(2,1)S(1)}, u32[]{:S(2)}, u32[]{:S(2)}) collective-permute-start(bf16[128,128]{1,0:T(8,128)(2,1)S(1)} %collective-permute-done.5), channel_id=1, source_target_pairs={{0,2},{2,4},{4,6},{6,8},{8,10},{10,12},{12,14},{14,16},{16,18},{18... | collective-permute-start | bytes 98312 | tf_op jit(solution)/shard_map/ppermute | solution.py:19
  50.0 6.0 %collective-permute-start.7 = (bf16[128,128]{1,0:T(8,128)(2,1)S(1)}, bf16[128,128]{1,0:T(8,128)(2,1)S(1)}, u32[]{:S(2)}, u32[]{:S(2)}) collective-permute-start(bf16[128,128]{1,0:T(8,128)(2,1)S(1)} %collective-permute-done.6), channel_id=1, source_target_pairs={{0,2},{2,4},{4,6},{6,8},{8,10},{10,12},{12,14},{14,16},{16,18},{18... | collective-permute-start | bytes 98312 | tf_op jit(solution)/shard_map/ppermute | solution.py:19
  56.1 6.0 %collective-permute-start.8 = (bf16[128,128]{1,0:T(8,128)(2,1)S(1)}, bf16[128,128]{1,0:T(8,128)(2,1)S(1)}, u32[]{:S(2)}, u32[]{:S(2)}) collective-permute-start(bf16[128,128]{1,0:T(8,128)(2,1)S(1)} %collective-permute-done.7), channel_id=1, source_target_pairs={{0,2},{2,4},{4,6},{6,8},{8,10},{10,12},{12,14},{14,16},{16,18},{18... | collective-permute-start | bytes 98312 | tf_op jit(solution)/shard_map/ppermute | solution.py:19
  62.1 6.0 %collective-permute-start.9 = (bf16[128,128]{1,0:T(8,128)(2,1)S(1)}, bf16[128,128]{1,0:T(8,128)(2,1)S(1)}, u32[]{:S(2)}, u32[]{:S(2)}) collective-permute-start(bf16[128,128]{1,0:T(8,128)(2,1)S(1)} %collective-permute-done.8), channel_id=1, source_target_pairs={{0,2},{2,4},{4,6},{6,8},{8,10},{10,12},{12,14},{14,16},{16,18},{18... | collective-permute-start | bytes 98312 | tf_op jit(solution)/shard_map/ppermute | solution.py:19
  68.2 6.0 %collective-permute-start.10 = (bf16[128,128]{1,0:T(8,128)(2,1)S(1)}, bf16[128,128]{1,0:T(8,128)(2,1)S(1)}, u32[]{:S(2)}, u32[]{:S(2)}) collective-permute-start(bf16[128,128]{1,0:T(8,128)(2,1)S(1)} %collective-permute-done.9), channel_id=1, source_target_pairs={{0,2},{2,4},{4,6},{6,8},{8,10},{10,12},{12,14},{14,16},{16,18},{18... | collective-permute-start | bytes 98312 | tf_op jit(solution)/shard_map/ppermute | solution.py:19
  74.2 6.0 %collective-permute-start.11 = (bf16[128,128]{1,0:T(8,128)(2,1)S(1)}, bf16[128,128]{1,0:T(8,128)(2,1)S(1)}, u32[]{:S(2)}, u32[]{:S(2)}) collective-permute-start(bf16[128,128]{1,0:T(8,128)(2,1)S(1)} %collective-permute-done.10), channel_id=1, source_target_pairs={{0,2},{2,4},{4,6},{6,8},{8,10},{10,12},{12,14},{14,16},{16,18},{18... | collective-permute-start | bytes 98312 | tf_op jit(solution)/shard_map/ppermute | solution.py:19
  80.2 6.0 %collective-permute-start.12 = (bf16[128,128]{1,0:T(8,128)(2,1)S(1)}, bf16[128,128]{1,0:T(8,128)(2,1)S(1)}, u32[]{:S(2)}, u32[]{:S(2)}) collective-permute-start(bf16[128,128]{1,0:T(8,128)(2,1)S(1)} %collective-permute-done.11), channel_id=1, source_target_pairs={{0,2},{2,4},{4,6},{6,8},{8,10},{10,12},{12,14},{14,16},{16,18},{18... | collective-permute-start | bytes 98312 | tf_op jit(solution)/shard_map/ppermute | solution.py:19
  86.3 6.0 %collective-permute-start.13 = (bf16[128,128]{1,0:T(8,128)(2,1)S(1)}, bf16[128,128]{1,0:T(8,128)(2,1)S(1)}, u32[]{:S(2)}, u32[]{:S(2)}) collective-permute-start(bf16[128,128]{1,0:T(8,128)(2,1)S(1)} %collective-permute-done.12), channel_id=1, source_target_pairs={{0,2},{2,4},{4,6},{6,8},{8,10},{10,12},{12,14},{14,16},{16,18},{18... | collective-permute-start | bytes 98312 | tf_op jit(solution)/shard_map/ppermute | solution.py:19
  92.3 6.0 %collective-permute-start.14 = (bf16[128,128]{1,0:T(8,128)(2,1)S(1)}, bf16[128,128]{1,0:T(8,128)(2,1)S(1)}, u32[]{:S(2)}, u32[]{:S(2)}) collective-permute-start(bf16[128,128]{1,0:T(8,128)(2,1)S(1)} %collective-permute-done.13), channel_id=1, source_target_pairs={{0,2},{2,4},{4,6},{6,8},{8,10},{10,12},{12,14},{14,16},{16,18},{18... | collective-permute-start | bytes 98312 | tf_op jit(solution)/shard_map/ppermute | solution.py:19
  103.0 0.7 copy-start.2
  103.1 8.9 %copy-start.3 = (bf16[128,128]{1,0:T(8,128)(2,1)S(1)}, bf16[128,128]{1,0:T(8,128)(2,1)}, u32[]{:S(2)}) copy-start(bf16[128,128]{1,0:T(8,128)(2,1)} %param.11) | copy-start | bytes 98308
Sparse Core Ops, SparseCore 0:
  103.8 8.0 reduce-scatter.1
